TPU v7x, 32 devices: a whole 2x2x4 slice. The times are simulated.
32 devices in a mesh: sc: 4 (over y, x), rows: 8 (over z, core).
Axes of the slice: x: 2, y: 2, z: 4, core: 2. Of those that a mesh axis runs over, the one named last changes fastest.
Arguments:
- embeddings: bfloat16 [32768, 1024], P(('sc', 'rows')), may hold values from -6 to 6
- labels: int32 [32768, 1], P(('sc', 'rows')), may hold values from 0 to 3; in each aligned block of 1024 rows (0 to 1023, 1024 to 2047, ...) at most 512 rows name the same one
- init_idx: int32 [4, 256], P('sc'), may hold values from 0 to 16383
Outputs:
- assign: bfloat16 [32768, 256], P(('sc', 'rows'))
- centroids: float32 [4, 256, 1024], P('sc')
Inputs may be any that keep to these rules, and one draw needn't show every extreme that they name: `labels`: among the rows of one device (aligned blocks of 1024 rows) no label occurs more than 512 times, and some label occurs exactly 512 times; every label occurs somewhere.
All inputs are finite; a program needn't handle non-finite values.
Results may differ from a plain program's by a relative error of at most 0.0052.
Values may be sent and summed in bfloat16 or wider, within the bound.
A program may use at most 64 MiB of HBM per device.

v0:
```python
import math
import jax
import jax.numpy as jnp
from jax import lax
from jax.sharding import PartitionSpec as P

ITERS = 3
ROUNDS = 3


def carried_in(part, axis, combine, identity):
    place = lax.axis_index(axis)
    gathered = lax.all_gather(part, axis)
    state = jnp.zeros_like(part) + jnp.asarray(identity, part.dtype)

    def one(turn, state):
        return combine(state, lax.dynamic_index_in_dim(gathered, turn, 0, False))

    return lax.fori_loop(0, place, one, state)


def unit_of(rows):
    values = rows.astype(jnp.float32)
    scale = lax.rsqrt(jnp.mean(values * values, axis=1, keepdims=True) + 1e-05) * (
        1.0 / math.sqrt(rows.shape[1])
    )
    return (values * scale).astype(jnp.bfloat16)


def unit_cent(mass):
    return (mass * lax.rsqrt(jnp.sum(mass * mass, axis=1, keepdims=True) + 1e-06)).astype(
        jnp.bfloat16
    )


def on_device(embeddings, labels, init_idx):
    tok = embeddings.shape[0]
    width = embeddings.shape[1]
    groups = lax.axis_size("sc")
    slots = 2 * tok // groups
    label_col = labels[:, 0]
    member = (label_col[:, None] == jnp.arange(groups, dtype=jnp.int32)[None, :]).astype(jnp.int32)
    before_here = jnp.cumsum(member, axis=0) - member
    place = jnp.sum(before_here * member, axis=1)
    counts = jnp.sum(member, axis=0).astype(jnp.float32)
    prefix = carried_in(
        counts, ("sc", "rows"), lambda early, later: early + later, jnp.zeros_like(counts)
    )
    totals = lax.psum(counts, ("sc", "rows"))
    prefix_int = prefix.astype(jnp.int32)
    totals_int = totals.astype(jnp.int32)
    rank = jnp.sum(member * prefix_int[None, :], axis=1) + place
    target = label_col * slots + place
    source = (
        jnp.full((groups * slots,), tok, jnp.int32).at[target].set(jnp.arange(tok, dtype=jnp.int32))
    )
    padded = jnp.concatenate([embeddings, jnp.zeros((1, width), jnp.bfloat16)], axis=0)
    rank_pad = jnp.concatenate([rank, jnp.full((1,), -1, jnp.int32)], axis=0)
    outgoing = padded[source].reshape(groups, slots, width)
    out_rank = rank_pad[source].reshape(groups, slots)
    incoming, in_rank = (
        lax.all_to_all(outgoing, "sc", split_axis=0, concat_axis=0, tiled=True),
        lax.all_to_all(out_rank, "sc", split_axis=0, concat_axis=0, tiled=True),
    )
    incoming = incoming.reshape(groups * slots, width)
    in_rank = in_rank.reshape(groups * slots)
    valid = in_rank >= 0
    members = unit_of(incoming)
    group_here = lax.axis_index("sc")
    count = jnp.sum(jnp.where(jnp.arange(groups, dtype=jnp.int32) == group_here, totals_int, 0))
    wanted = init_idx[0] % count
    picker = (wanted[:, None] == in_rank[None, :]).astype(jnp.bfloat16)
    seeds = jnp.dot(picker, members, preferred_element_type=jnp.float32)
    cent = lax.psum(seeds, "rows").astype(jnp.bfloat16)
    contract_rows = (((0,), (0,)), ((), ()))
    contract_width = (((1,), (1,)), ((), ()))
    for round_index in range(ROUNDS):
        scores = lax.dot_general(members, cent, contract_width, preferred_element_type=jnp.float32)
        plan = jnp.where(valid[:, None], jnp.exp(scores * 10.0), 0.0)
        for step in range(ITERS):
            column = lax.psum(jnp.sum(plan, axis=0), "rows")
            plan = plan / column[None, :]
            row_sum = jnp.sum(plan, axis=1)
            plan = jnp.where(valid[:, None], plan / jnp.where(valid, row_sum, 1.0)[:, None], 0.0)
        plan_b = plan.astype(jnp.bfloat16)
        mass_part = lax.dot_general(
            plan_b, members, contract_rows, preferred_element_type=jnp.float32
        )
        if round_index < ROUNDS - 1:
            mass = lax.psum(mass_part, "rows")
            cent = unit_cent(mass)
        else:
            weight_part = jnp.sum(plan, axis=0)
            mass, weight = lax.psum((mass_part, weight_part), "rows")
            means = mass / weight[:, None]
    plan_out = plan.astype(jnp.bfloat16).reshape(groups, slots, plan.shape[1])
    returned = lax.all_to_all(plan_out, "sc", split_axis=0, concat_axis=0, tiled=True).reshape(
        groups * slots, plan.shape[1]
    )
    assign = returned[target]
    return (assign, means[None])


def solution(mesh):
    return jax.shard_map(
        on_device,
        mesh=mesh,
        in_specs=(P(("sc", "rows"), None), P(("sc", "rows"), None), P("sc", None)),
        out_specs=(P(("sc", "rows"), None), P("sc", None, None)),
        check_vma=False,
    )
```

profile of v0, /device:TPU:0, one launch (start us, length us, event | category | flops | bytes accessed | tf_op | source)
XLA Modules:
  0.0 568.7 jit_solution(1118507430221130394)
XLA Ops:
  8.1 42.0 %all-reduce.2 = (f32[128]{0:T(128)S(1)}, f32[4]{0:T(128)S(1)}) all-reduce(f32[128]{0:T(128)S(1)} %convert_dynamic-update-slice_fusion, f32[4]{0:T(128)S(1)} %convert_element_type.59), channel_id=2, replica_groups=mesh['sc'=4,'rows'=8] {'sc','rows'}, use_global_device_ids=true, to_apply=%add.1 | all-reduce | flops 132 | bytes 1056
  54.0 4.3 scatter_custom_fusion
  58.4 20.6 %gather_fusion = s32[2048]{0:T(1024)} fusion(s32[1025]{0:T(1024)S(1)} %pad_add_fusion, s32[2048]{0:T(1024)S(1)} %fusion.27), kind=kCustom, calls=%fused_computation | custom fusion | bytes 24576 | tf_op jit(solution)/shard_map/gather | solution.py:60
  78.9 4.4 all-to-all-start
  85.1 9.7 %gather_fusion.1 = bf16[2048,1024]{1,0:T(8,128)(2,1)} fusion(bf16[1025,1024]{1,0:T(8,128)(2,1)S(1)} %concatenate.7, s32[2048]{0:T(1024)S(1)} %fusion.27), kind=kCustom, calls=%fused_computation.1 | custom fusion | bytes 8396800 | tf_op jit(solution)/shard_map/gather | solution.py:59
  94.8 5.0 all-to-all-start.1
  101.9 44.5 %all-to-all-done.1 = bf16[4,512,1024]{2,1,0:T(8,128)(2,1)} async-done(((bf16[4,512,1024]{2,1,0:T(8,128)(2,1)}), bf16[4,512,1024]{2,1,0:T(8,128)(2,1)}, u32[]{:S(2)}, u32[]{:S(2)}) %all-to-all-start.1) | async-done | bytes 4194336 | tf_op jit(solution)/shard_map/all_to_all | solution.py:62
  155.8 57.9 %all-reduce.13 = bf16[256,1024]{1,0:T(8,128)(2,1)S(1)} all-reduce(f32[256,1024]{1,0:T(8,128)S(1)} %fusion.7), channel_id=1, replica_groups=mesh['sc'=4,'rows'=8] {'rows'}, use_global_device_ids=true, to_apply=%region_11.12 | all-reduce | flops 262144 | bytes 1572864 | tf_op jit(solution)/shard_map/psum | solution.py:74
  216.8 15.1 %psum.107 = f32[256]{0:T(256)S(1)} all-reduce(f32[256]{0:T(256)S(1)} %get-tuple-element.52), channel_id=1, replica_groups=mesh['sc'=4,'rows'=8] {'rows'}, use_global_device_ids=true, to_apply=%region_13.14 | all-reduce | flops 256 | bytes 2048 | tf_op jit(solution)/shard_map/psum | solution.py:81
  234.3 13.6 %psum.108 = f32[256]{0:T(256)S(1)} all-reduce(f32[256]{0:T(256)S(1)} %get-tuple-element.48), channel_id=1, replica_groups=mesh['sc'=4,'rows'=8] {'rows'}, use_global_device_ids=true, to_apply=%region_16.17 | all-reduce | flops 256 | bytes 2048 | tf_op jit(solution)/shard_map/psum | solution.py:81
  250.0 13.7 %psum.109 = f32[256]{0:T(256)S(1)} all-reduce(f32[256]{0:T(256)S(1)} %get-tuple-element.46), channel_id=1, replica_groups=mesh['sc'=4,'rows'=8] {'rows'}, use_global_device_ids=true, to_apply=%region_19.20 | all-reduce | flops 256 | bytes 2048 | tf_op jit(solution)/shard_map/psum | solution.py:81
  265.7 4.9 fusion.9
  270.9 56.0 %all-reduce.8.cloned.1.call-done = f32[256,1024]{1,0:T(8,128)} async-done(((f32[256,1024]{1,0:T(8,128)}), f32[256,1024]{1,0:T(8,128)}) %all-reduce.8.cloned.1.call-update) | async-done | bytes 1048592 | tf_op jit(solution)/shard_map/psum | solution.py:90
  331.8 13.6 %psum.111 = f32[256]{0:T(256)S(1)} all-reduce(f32[256]{0:T(256)S(1)} %get-tuple-element.54), channel_id=1, replica_groups=mesh['sc'=4,'rows'=8] {'rows'}, use_global_device_ids=true, to_apply=%region_24.25 | all-reduce | flops 256 | bytes 2048 | tf_op jit(solution)/shard_map/psum | solution.py:81
  347.7 13.6 %psum.112 = f32[256]{0:T(256)S(1)} all-reduce(f32[256]{0:T(256)S(1)} %get-tuple-element.44), channel_id=1, replica_groups=mesh['sc'=4,'rows'=8] {'rows'}, use_global_device_ids=true, to_apply=%region_27.28 | all-reduce | flops 256 | bytes 2048 | tf_op jit(solution)/shard_map/psum | solution.py:81
  363.4 13.7 %psum.113 = f32[256]{0:T(256)S(1)} all-reduce(f32[256]{0:T(256)S(1)} %get-tuple-element.42), channel_id=1, replica_groups=mesh['sc'=4,'rows'=8] {'rows'}, use_global_device_ids=true, to_apply=%region_30.31 | all-reduce | flops 256 | bytes 2048 | tf_op jit(solution)/shard_map/psum | solution.py:81
  379.1 4.9 fusion.10
  384.1 57.0 %all-reduce.10.cloned.1.call-done = f32[256,1024]{1,0:T(8,128)} async-done(((f32[256,1024]{1,0:T(8,128)}), f32[256,1024]{1,0:T(8,128)}) %all-reduce.10.cloned.1.call-update) | async-done | bytes 1048592 | tf_op jit(solution)/shard_map/psum | solution.py:90
  446.1 13.6 %psum.115 = f32[256]{0:T(256)S(1)} all-reduce(f32[256]{0:T(256)S(1)} %get-tuple-element.56), channel_id=1, replica_groups=mesh['sc'=4,'rows'=8] {'rows'}, use_global_device_ids=true, to_apply=%region_35.36 | all-reduce | flops 256 | bytes 2048 | tf_op jit(solution)/shard_map/psum | solution.py:81
  462.1 13.6 %psum.116 = f32[256]{0:T(256)S(1)} all-reduce(f32[256]{0:T(256)S(1)} %get-tuple-element.40), channel_id=1, replica_groups=mesh['sc'=4,'rows'=8] {'rows'}, use_global_device_ids=true, to_apply=%region_38.39 | all-reduce | flops 256 | bytes 2048 | tf_op jit(solution)/shard_map/psum | solution.py:81
  478.0 13.6 %psum.117 = f32[256]{0:T(256)S(1)} all-reduce(f32[256]{0:T(256)S(1)} %get-tuple-element.38), channel_id=1, replica_groups=mesh['sc'=4,'rows'=8] {'rows'}, use_global_device_ids=true, to_apply=%region_41.42 | all-reduce | flops 256 | bytes 2048 | tf_op jit(solution)/shard_map/psum | solution.py:81
  501.3 13.9 %psum.119 = f32[256]{0:T(256)S(1)} all-reduce(f32[256]{0:T(256)S(1)} %get-tuple-element.50), channel_id=1, replica_groups=mesh['sc'=4,'rows'=8] {'rows'}, use_global_device_ids=true, to_apply=%region_45.46 | all-reduce | flops 256 | bytes 2048 | tf_op jit(solution)/shard_map/psum | solution.py:94
  515.2 39.6 %all-reduce.12.cloned.1.call-done = f32[256,1024]{1,0:T(8,128)} async-done(((f32[256,1024]{1,0:T(8,128)}), f32[256,1024]{1,0:T(8,128)}) %all-reduce.12.cloned.1.call-update) | async-done | bytes 1048592 | tf_op jit(solution)/shard_map/psum | solution.py:94
  557.2 5.0 gather_fusion.2
  (91 shorter events, 59.4 us)
Async XLA Ops:
  78.9 15.9 %all-to-all-start = ((s32[4,1,512]{2,1,0:T(1,128)}), s32[4,1,512]{2,1,0:T(1,128)S(1)}, u32[]{:S(2)}, u32[]{:S(2)}) async-start(s32[4,1,512]{2,1,0:T(1,128)} %bitcast.6), calls=%async_computation | async-start | bytes 16384 | tf_op jit(solution)/shard_map/all_to_all | solution.py:63
  94.8 7.0 %copy-start.8 = (s32[1,256]{1,0:T(1,128)S(1)}, s32[1,256]{1,0:T(1,128)}, u32[]{:S(2)}) copy-start(s32[1,256]{1,0:T(1,128)} %param.7) | copy-start | bytes 3076
  94.8 51.7 %all-to-all-start.1 = ((bf16[4,512,1024]{2,1,0:T(8,128)(2,1)}), bf16[4,512,1024]{2,1,0:T(8,128)(2,1)}, u32[]{:S(2)}, u32[]{:S(2)}) async-start(bf16[4,512,1024]{2,1,0:T(8,128)(2,1)} %bitcast.45), calls=%async_computation.1 | async-start | bytes 8388608 | tf_op jit(solution)/shard_map/all_to_all | solution.py:62
  99.8 227.1 %all-reduce.8.cloned.1.call-start = ((), (), s32[]{:S(2)}) async-start(), calls=%async_computation.3 | async-start | bytes 2097152 | tf_op jit(solution)/shard_map/psum | solution.py:90
  152.5 1.9 copy-start.6
  216.8 15.5 %copy-start.3 = (f32[2048,256]{1,0:T(8,128)}, f32[2048,256]{1,0:T(8,128)S(1)}, u32[]{:S(2)}) copy-start(f32[2048,256]{1,0:T(8,128)S(1)} %get-tuple-element.53) | copy-start | bytes 6291460
  250.0 15.7 %copy-start.4 = (f32[2048,256]{1,0:T(8,128)S(1)}, f32[2048,256]{1,0:T(8,128)}, u32[]{:S(2)}) copy-start(f32[2048,256]{1,0:T(8,128)} %get-tuple-element.47) | copy-start | bytes 6291460
  270.6 170.5 %all-reduce.10.cloned.1.call-start = ((), (), s32[]{:S(2)}) async-start(), calls=%async_computation.4 | async-start | bytes 2097152 | tf_op jit(solution)/shard_map/psum | solution.py:90
  331.8 14.0 %copy-start.1 = (f32[2048,256]{1,0:T(8,128)}, f32[2048,256]{1,0:T(8,128)S(1)}, u32[]{:S(2)}) copy-start(f32[2048,256]{1,0:T(8,128)S(1)} %get-tuple-element.55) | copy-start | bytes 6291460
  363.4 15.7 %copy-start.5 = (f32[2048,256]{1,0:T(8,128)S(1)}, f32[2048,256]{1,0:T(8,128)}, u32[]{:S(2)}) copy-start(f32[2048,256]{1,0:T(8,128)} %get-tuple-element.43) | copy-start | bytes 6291460
  384.1 170.8 %all-reduce.12.cloned.1.call-start = ((), (), s32[]{:S(2)}) async-start(), calls=%async_computation.5 | async-start | bytes 2097152 | tf_op jit(solution)/shard_map/psum | solution.py:94
  446.1 14.0 %copy-start.2 = (f32[2048,256]{1,0:T(8,128)}, f32[2048,256]{1,0:T(8,128)S(1)}, u32[]{:S(2)}) copy-start(f32[2048,256]{1,0:T(8,128)S(1)} %get-tuple-element.57) | copy-start | bytes 6291460
  462.1 14.0 %copy-start = (f32[2048,256]{1,0:T(8,128)}, f32[2048,256]{1,0:T(8,128)S(1)}, u32[]{:S(2)}) copy-start(f32[2048,256]{1,0:T(8,128)S(1)} %get-tuple-element.41) | copy-start | bytes 6291460
  491.6 2.6 copy-start.7
  497.7 59.5 %all-to-all-start.2 = ((bf16[4,512,256]{2,1,0:T(8,128)(2,1)}), bf16[4,512,256]{2,1,0:T(8,128)(2,1)S(1)}, u32[]{:S(2)}, u32[]{:S(2)}) async-start(bf16[4,512,256]{2,1,0:T(8,128)(2,1)} %bitcast.11), calls=%async_computation.2 | async-start | bytes 2097152 | tf_op jit(solution)/shard_map/all_to_all | solution.py:97
Sparse Core Ops, SparseCore 0:
  270.8 56.0 all-reduce.7
  384.2 56.9 all-reduce.9
  497.8 56.9 all-reduce.11
where the time goes:
time: 570 us; the launch traced here: 569 us
  blocking collectives  238 us (42%)
  waiting for transfers between devices  197 us (35%)
  local copies, waits for them, and re-layouts  44.2 us (8%)
  other arithmetic  35.6 us (6%)
  matrix products  25 us (4%)
  between operations  15.5 us (3%)
  starting transfers between devices  13.4 us (2%)
    psum x9, blocking collectives, on_device(): column = lax.psum(jnp.sum(plan, axis=0), 'rows')  124 us
    psum x2, waiting for transfers between devices, on_device(): mass = lax.psum(mass_part, 'rows')  113 us
    psum x1, blocking collectives, on_device(): cent = lax.psum(seeds, 'rows').astype(jnp.bfloat16)  57.9 us
    all_to_all x1, waiting for transfers between devices, on_device(): lax.all_to_all(outgoing, 'sc', split_axis=0, concat_axis=0, tiled=True)  44.5 us
    unnamed x1, blocking collectives  42 us
    psum x1, waiting for transfers between devices, on_device(): mass, weight = lax.psum((mass_part, weight_part), 'rows')  39.6 us
    gather x1, local copies, waits for them, and re-layouts, on_device(): out_rank = rank_pad[source].reshape(groups, slots)  20.6 us
    psum x1, blocking collectives, on_device(): mass, weight = lax.psum((mass_part, weight_part), 'rows')  13.9 us
  transfers between devices with their start and end apart: 6, of which 4 were waited for; matrix products, arithmetic and copies ran while one was open for 3% of the time, Pallas kernels for 0%

commit v1 on v0

--- a/solution.py
+++ b/solution.py
@@ -6,6 +6,18 @@
 
 ITERS = 3
 ROUNDS = 3
+
+
+def exchange_directly(shard, axis, split, join):
+    ways, here = (lax.axis_size(axis), lax.axis_index(axis))
+    width = shard.shape[split] // ways
+    turned = jnp.roll(shard, -here * width, axis=split)
+    got = [lax.slice_in_dim(turned, 0, width, axis=split)]
+    for far in range(1, ways):
+        sent = lax.slice_in_dim(turned, far * width, (far + 1) * width, axis=split)
+        got.append(lax.ppermute(sent, axis, [(d, (d + far) % ways) for d in range(ways)]))
+    line = jnp.concatenate(got[::-1], axis=join)
+    return jnp.roll(line, (here + 1) * got[0].shape[join], axis=join)
 
 
 def carried_in(part, axis, combine, identity):
@@ -59,7 +71,7 @@
     outgoing = padded[source].reshape(groups, slots, width)
     out_rank = rank_pad[source].reshape(groups, slots)
     incoming, in_rank = (
-        lax.all_to_all(outgoing, "sc", split_axis=0, concat_axis=0, tiled=True),
+        exchange_directly(outgoing, "sc", 0, 0),
         lax.all_to_all(out_rank, "sc", split_axis=0, concat_axis=0, tiled=True),
     )
     incoming = incoming.reshape(groups * slots, width)

time: 570 us -> 550 us (0.965)
  waiting for transfers between devices: 197 us -> 172 us
    all_to_all x1 -> x0, waiting for transfers between devices: 44.5 us -> none  [on_device(): lax.all_to_all(outgoing, 'sc', split_axis=0, concat_axis=0, tiled=True)]
    all_to_all x1, waiting for transfers between devices: 0.01 us -> 19 us  [on_device(): lax.all_to_all(out_rank, 'sc', split_axis=0, concat_axis=0, tiled=True)]
  transfers between devices with their start and end apart: 6 -> 8, of which waited for: 4 -> 4; matrix products, arithmetic and copies ran while one was open for 3% -> 4% of each run, Pallas kernels for 0% -> 0%
where the time goes in v1:
time: 550 us; the launch traced here: 549 us
  blocking collectives  238 us (43%)
  waiting for transfers between devices  172 us (31%)
  local copies, waits for them, and re-layouts  46 us (8%)
  other arithmetic  40.6 us (7%)
  matrix products  25 us (5%)
  between operations  15.3 us (3%)
  starting transfers between devices  11.9 us (2%)
    psum x9, blocking collectives, on_device(): column = lax.psum(jnp.sum(plan, axis=0), 'rows')  124 us
    psum x2, waiting for transfers between devices, on_device(): mass = lax.psum(mass_part, 'rows')  114 us
    psum x1, blocking collectives, on_device(): cent = lax.psum(seeds, 'rows').astype(jnp.bfloat16)  57.8 us
    unnamed x1, blocking collectives  42 us
    psum x1, waiting for transfers between devices, on_device(): mass, weight = lax.psum((mass_part, weight_part), 'rows')  39.6 us
    gather x1, local copies, waits for them, and re-layouts, on_device(): out_rank = rank_pad[source].reshape(groups, slots)  20.6 us
    all_to_all x1, waiting for transfers between devices, on_device(): lax.all_to_all(out_rank, 'sc', split_axis=0, concat_axis=0, tiled=True)  19 us
    psum x1, blocking collectives, on_device(): mass, weight = lax.psum((mass_part, weight_part), 'rows')  13.9 us
  transfers between devices with their start and end apart: 8, of which 4 were waited for; matrix products, arithmetic and copies ran while one was open for 4% of the time, Pallas kernels for 0%

profile of v1, /device:TPU:0, one launch (start us, length us, event | category | flops | bytes accessed | tf_op | source)
XLA Modules:
  0.0 549.2 jit_solution(15746547357838925265)
XLA Ops:
  8.1 42.0 %all-reduce.2 = (f32[128]{0:T(128)S(1)}, f32[4]{0:T(128)S(1)}) all-reduce(f32[128]{0:T(128)S(1)} %convert_dynamic-update-slice_fusion, f32[4]{0:T(128)S(1)} %convert_element_type.59), channel_id=2, replica_groups=mesh['sc'=4,'rows'=8] {'sc','rows'}, use_global_device_ids=true, to_apply=%add.1 | all-reduce | flops 132 | bytes 1056
  54.0 4.3 scatter_custom_fusion
  60.1 9.7 %gather_fusion.1 = bf16[2048,1024]{1,0:T(8,128)(2,1)} fusion(bf16[1025,1024]{1,0:T(8,128)(2,1)S(1)} %concatenate.13, s32[2048]{0:T(1024)S(1)} %fusion.36), kind=kCustom, calls=%fused_computation.1 | custom fusion | bytes 8396800 | tf_op jit(solution)/shard_map/gather | solution.py:71
  79.6 20.6 %gather_fusion = s32[2048]{0:T(1024)} fusion(s32[1025]{0:T(1024)S(1)} %pad_add_fusion, s32[2048]{0:T(1024)S(1)} %fusion.36), kind=kCustom, calls=%fused_computation | custom fusion | bytes 24576 | tf_op jit(solution)/shard_map/gather | solution.py:72
  105.4 19.0 %all-to-all-done = s32[4,1,512]{2,1,0:T(1,128)S(1)} async-done(((s32[4,1,512]{2,1,0:T(1,128)}), s32[4,1,512]{2,1,0:T(1,128)S(1)}, u32[]{:S(2)}, u32[]{:S(2)}) %all-to-all-start) | async-done | bytes 8224 | tf_op jit(solution)/shard_map/all_to_all | solution.py:75
  124.4 7.5 %multiply_reduce_fusion = (f32[4,512]{1,0:T(4,128)S(1)}, f32[4,512,1024]{2,1,0:T(8,128)S(1)}) fusion(s32[]{:T(128)S(6)} %select_n.171, bf16[1,512,1024]{2,1,0:T(8,128)(2,1)S(1)} %get-tuple-element.56, bf16[1,512,1024]{2,1,0:T(8,128)(2,1)} %collective-permute-done.2, bf16[1,512,1024]{2,1,0:T(8,128)(2,1)} %collective-permute-done.1, ...), kind=kLoop, calls=%fused_computation.17 | loop fusion | flops 20969472 | bytes 12591108 | tf_op jit(solution)/shard_map/reduce_sum | solution.py:36
  135.6 57.8 %all-reduce.13 = bf16[256,1024]{1,0:T(8,128)(2,1)S(1)} all-reduce(f32[256,1024]{1,0:T(8,128)S(1)} %fusion.16), channel_id=1, replica_groups=mesh['sc'=4,'rows'=8] {'rows'}, use_global_device_ids=true, to_apply=%region_11.13 | all-reduce | flops 262144 | bytes 1572864 | tf_op jit(solution)/shard_map/psum | solution.py:86
  196.6 15.3 %psum.107 = f32[256]{0:T(256)S(1)} all-reduce(f32[256]{0:T(256)S(1)} %get-tuple-element.59), channel_id=1, replica_groups=mesh['sc'=4,'rows'=8] {'rows'}, use_global_device_ids=true, to_apply=%region_13.15 | all-reduce | flops 256 | bytes 2048 | tf_op jit(solution)/shard_map/psum | solution.py:93
  214.2 13.6 %psum.108 = f32[256]{0:T(256)S(1)} all-reduce(f32[256]{0:T(256)S(1)} %get-tuple-element.49), channel_id=1, replica_groups=mesh['sc'=4,'rows'=8] {'rows'}, use_global_device_ids=true, to_apply=%region_16.18 | all-reduce | flops 256 | bytes 2048 | tf_op jit(solution)/shard_map/psum | solution.py:93
  229.9 13.9 %psum.109 = f32[256]{0:T(256)S(1)} all-reduce(f32[256]{0:T(256)S(1)} %get-tuple-element.47), channel_id=1, replica_groups=mesh['sc'=4,'rows'=8] {'rows'}, use_global_device_ids=true, to_apply=%region_19.21 | all-reduce | flops 256 | bytes 2048 | tf_op jit(solution)/shard_map/psum | solution.py:93
  245.7 4.9 fusion.18
  250.7 56.6 %all-reduce.8.cloned.1.call-done = f32[256,1024]{1,0:T(8,128)} async-done(((f32[256,1024]{1,0:T(8,128)}), f32[256,1024]{1,0:T(8,128)}) %all-reduce.8.cloned.1.call-update) | async-done | bytes 1048592 | tf_op jit(solution)/shard_map/psum | solution.py:102
  312.3 13.6 %psum.111 = f32[256]{0:T(256)S(1)} all-reduce(f32[256]{0:T(256)S(1)} %get-tuple-element.61), channel_id=1, replica_groups=mesh['sc'=4,'rows'=8] {'rows'}, use_global_device_ids=true, to_apply=%region_24.26 | all-reduce | flops 256 | bytes 2048 | tf_op jit(solution)/shard_map/psum | solution.py:93
  328.2 13.6 %psum.112 = f32[256]{0:T(256)S(1)} all-reduce(f32[256]{0:T(256)S(1)} %get-tuple-element.45), channel_id=1, replica_groups=mesh['sc'=4,'rows'=8] {'rows'}, use_global_device_ids=true, to_apply=%region_27.29 | all-reduce | flops 256 | bytes 2048 | tf_op jit(solution)/shard_map/psum | solution.py:93
  343.9 13.7 %psum.113 = f32[256]{0:T(256)S(1)} all-reduce(f32[256]{0:T(256)S(1)} %get-tuple-element.43), channel_id=1, replica_groups=mesh['sc'=4,'rows'=8] {'rows'}, use_global_device_ids=true, to_apply=%region_30.32 | all-reduce | flops 256 | bytes 2048 | tf_op jit(solution)/shard_map/psum | solution.py:93
  359.6 4.9 fusion.19
  364.6 57.1 %all-reduce.10.cloned.1.call-done = f32[256,1024]{1,0:T(8,128)} async-done(((f32[256,1024]{1,0:T(8,128)}), f32[256,1024]{1,0:T(8,128)}) %all-reduce.10.cloned.1.call-update) | async-done | bytes 1048592 | tf_op jit(solution)/shard_map/psum | solution.py:102
  426.7 13.6 %psum.115 = f32[256]{0:T(256)S(1)} all-reduce(f32[256]{0:T(256)S(1)} %get-tuple-element.63), channel_id=1, replica_groups=mesh['sc'=4,'rows'=8] {'rows'}, use_global_device_ids=true, to_apply=%region_35.37 | all-reduce | flops 256 | bytes 2048 | tf_op jit(solution)/shard_map/psum | solution.py:93
  442.6 13.6 %psum.116 = f32[256]{0:T(256)S(1)} all-reduce(f32[256]{0:T(256)S(1)} %get-tuple-element.41), channel_id=1, replica_groups=mesh['sc'=4,'rows'=8] {'rows'}, use_global_device_ids=true, to_apply=%region_38.40 | all-reduce | flops 256 | bytes 2048 | tf_op jit(solution)/shard_map/psum | solution.py:93
  458.6 13.6 %psum.117 = f32[256]{0:T(256)S(1)} all-reduce(f32[256]{0:T(256)S(1)} %get-tuple-element.39), channel_id=1, replica_groups=mesh['sc'=4,'rows'=8] {'rows'}, use_global_device_ids=true, to_apply=%region_41.43 | all-reduce | flops 256 | bytes 2048 | tf_op jit(solution)/shard_map/psum | solution.py:93
  478.2 3.6 all-to-all-start.1
  481.9 13.9 %psum.119 = f32[256]{0:T(256)S(1)} all-reduce(f32[256]{0:T(256)S(1)} %get-tuple-element.57), channel_id=1, replica_groups=mesh['sc'=4,'rows'=8] {'rows'}, use_global_device_ids=true, to_apply=%region_45.47 | all-reduce | flops 256 | bytes 2048 | tf_op jit(solution)/shard_map/psum | solution.py:106
  495.8 39.6 %all-reduce.12.cloned.1.call-done = f32[256,1024]{1,0:T(8,128)} async-done(((f32[256,1024]{1,0:T(8,128)}), f32[256,1024]{1,0:T(8,128)}) %all-reduce.12.cloned.1.call-update) | async-done | bytes 1048592 | tf_op jit(solution)/shard_map/psum | solution.py:106
  537.7 5.0 gather_fusion.2
  (97 shorter events, 63.1 us)
Async XLA Ops:
  74.7 49.6 %collective-permute-start = (bf16[1,512,1024]{2,1,0:T(8,128)(2,1)}, bf16[1,512,1024]{2,1,0:T(8,128)(2,1)S(1)}, u32[]{:S(2)}, u32[]{:S(2)}) collective-permute-start(bf16[1,512,1024]{2,1,0:T(8,128)(2,1)} %get-tuple-element.53), channel_id=1, source_target_pairs={{0,24},{8,0},{16,8},{24,16},{1,25},{9,1},{17,9},{25,17},{2,26},{10... | collective-permute-start | bytes 3145736 | tf_op jit(solution)/shard_map/ppermute | solution.py:18
  77.8 46.5 %collective-permute-start.2 = (bf16[1,512,1024]{2,1,0:T(8,128)(2,1)}, bf16[1,512,1024]{2,1,0:T(8,128)(2,1)}, u32[]{:S(2)}, u32[]{:S(2)}) collective-permute-start(bf16[1,512,1024]{2,1,0:T(8,128)(2,1)} %get-tuple-element.54), channel_id=1, source_target_pairs={{0,8},{8,16},{16,24},{24,0},{1,9},{9,17},{17,25},{25,1},{2,10},{10... | collective-permute-start | bytes 3145736 | tf_op jit(solution)/shard_map/ppermute | solution.py:18
  77.8 46.5 %collective-permute-start.1 = (bf16[1,512,1024]{2,1,0:T(8,128)(2,1)S(1)}, bf16[1,512,1024]{2,1,0:T(8,128)(2,1)}, u32[]{:S(2)}, u32[]{:S(2)}) collective-permute-start(bf16[1,512,1024]{2,1,0:T(8,128)(2,1)S(1)} %get-tuple-element.55), channel_id=1, source_target_pairs={{0,16},{8,24},{16,0},{24,8},{1,17},{9,25},{17,1},{25,9},{2,18},{10... | collective-permute-start | bytes 3145736 | tf_op jit(solution)/shard_map/ppermute | solution.py:18
  79.6 25.6 %copy-start.8 = (s32[1,256]{1,0:T(1,128)S(1)}, s32[1,256]{1,0:T(1,128)}, u32[]{:S(2)}) copy-start(s32[1,256]{1,0:T(1,128)} %param.9) | copy-start | bytes 3076
  100.2 24.2 %all-to-all-start = ((s32[4,1,512]{2,1,0:T(1,128)}), s32[4,1,512]{2,1,0:T(1,128)S(1)}, u32[]{:S(2)}, u32[]{:S(2)}) async-start(s32[4,1,512]{2,1,0:T(1,128)} %bitcast.6), calls=%async_computation | async-start | bytes 16384 | tf_op jit(solution)/shard_map/all_to_all | solution.py:75
  103.5 203.8 %all-reduce.8.cloned.1.call-start = ((), (), s32[]{:S(2)}) async-start(), calls=%async_computation.2 | async-start | bytes 2097152 | tf_op jit(solution)/shard_map/psum | solution.py:102
  132.4 1.9 copy-start.6
  196.6 15.6 %copy-start.3 = (f32[2048,256]{1,0:T(8,128)}, f32[2048,256]{1,0:T(8,128)S(1)}, u32[]{:S(2)}) copy-start(f32[2048,256]{1,0:T(8,128)S(1)} %get-tuple-element.60) | copy-start | bytes 6291460
  229.9 15.8 %copy-start.4 = (f32[2048,256]{1,0:T(8,128)S(1)}, f32[2048,256]{1,0:T(8,128)}, u32[]{:S(2)}) copy-start(f32[2048,256]{1,0:T(8,128)} %get-tuple-element.48) | copy-start | bytes 6291460
  250.7 171.0 %all-reduce.10.cloned.1.call-start = ((), (), s32[]{:S(2)}) async-start(), calls=%async_computation.3 | async-start | bytes 2097152 | tf_op jit(solution)/shard_map/psum | solution.py:102
  312.3 14.0 %copy-start.1 = (f32[2048,256]{1,0:T(8,128)}, f32[2048,256]{1,0:T(8,128)S(1)}, u32[]{:S(2)}) copy-start(f32[2048,256]{1,0:T(8,128)S(1)} %get-tuple-element.62) | copy-start | bytes 6291460
  343.9 15.7 %copy-start.5 = (f32[2048,256]{1,0:T(8,128)S(1)}, f32[2048,256]{1,0:T(8,128)}, u32[]{:S(2)}) copy-start(f32[2048,256]{1,0:T(8,128)} %get-tuple-element.44) | copy-start | bytes 6291460
  364.5 170.8 %all-reduce.12.cloned.1.call-start = ((), (), s32[]{:S(2)}) async-start(), calls=%async_computation.4 | async-start | bytes 2097152 | tf_op jit(solution)/shard_map/psum | solution.py:106
  426.7 14.0 %copy-start.2 = (f32[2048,256]{1,0:T(8,128)}, f32[2048,256]{1,0:T(8,128)S(1)}, u32[]{:S(2)}) copy-start(f32[2048,256]{1,0:T(8,128)S(1)} %get-tuple-element.64) | copy-start | bytes 6291460
  442.6 14.0 %copy-start = (f32[2048,256]{1,0:T(8,128)}, f32[2048,256]{1,0:T(8,128)S(1)}, u32[]{:S(2)}) copy-start(f32[2048,256]{1,0:T(8,128)S(1)} %get-tuple-element.42) | copy-start | bytes 6291460
  472.2 2.6 copy-start.7
  478.2 59.5 %all-to-all-start.1 = ((bf16[4,512,256]{2,1,0:T(8,128)(2,1)}), bf16[4,512,256]{2,1,0:T(8,128)(2,1)S(1)}, u32[]{:S(2)}, u32[]{:S(2)}) async-start(bf16[4,512,256]{2,1,0:T(8,128)(2,1)} %bitcast.11), calls=%async_computation.1 | async-start | bytes 2097152 | tf_op jit(solution)/shard_map/all_to_all | solution.py:109
Sparse Core Ops, SparseCore 0:
  250.8 56.4 all-reduce.7
  364.7 56.9 all-reduce.9
  478.4 56.9 all-reduce.11
